TPU v7x, 256 devices: a whole 4x4x8 slice. The times are simulated.
256 devices in a mesh: atom: 32 (over y, z_hi, core), sample: 8 (over z_lo, x).
Axes of the slice: x: 4, y: 4, z: 8 (z_hi: 4, z_lo: 2; z = z_hi * 2 + z_lo), core: 2. Of those that a mesh axis runs over, the one named last changes fastest.
Arguments:
- atom_act: bfloat16 [16, 8192, 128], P('sample', 'atom'), may hold values from -3 to 3
- atom_cond: bfloat16 [8192, 128], P('atom'), may hold values from -6 to 6
- ref_pos: float32 [3, 8192], P(None, 'atom'), may hold values from -9 to 9
- atom_token: int32 [8192], P('atom'), may hold values from 0 to 340, never falling along the last dimension, each value on 1 to 48 neighbouring positions
- w_pair_in: float32 [16, 5], replicated, may hold values from -2.5 to 2.5
- w_rel: float32 [16, 9], replicated, may hold values from -6 to 6
- w_cond_pair: bfloat16 [2, 128, 16], replicated, may hold values from -1 to 1
- w_pair_mlp: float32 [3, 16, 16], replicated, may hold values from -1.5 to 1.5
- w_bias: float32 [3, 4, 16], replicated, may hold values from -6 to 6
- w_cond: bfloat16 [3, 128, 768], replicated, may hold values from -0.5 to 0.5
- w_attn: bfloat16 [3, 128, 512], replicated, may hold values from -0.5 to 0.5
- q_bias: float32 [3, 128], replicated, may hold values from -48 to 48
- w_out: bfloat16 [3, 128, 128], replicated, may hold values from -1 to 1
- w_up: bfloat16 [3, 128, 512], replicated, may hold values from -0.5 to 0.5
- w_down: bfloat16 [3, 256, 128], replicated, may hold values from -0.375 to 0.375
Outputs:
- atom_out: bfloat16 [16, 8192, 128], P('sample', 'atom')
Inputs may be any that keep to these rules, and one draw needn't show every extreme that they name: `atom_token`: atoms of one token are consecutive and token numbers never fall along the atoms; a token has 1 to 48 atoms.
All inputs are finite; a program needn't handle non-finite values.
Results may differ from a plain program's by a relative error of at most 0.023.
The roundings to bfloat16 on the way count: a program that leaves them out, or rounds other values in their place, can miss the bound.
Values may be sent and summed in bfloat16 or wider, within the bound.
A program may use at most 64 MiB of HBM per device.

v0:
```python
import jax
import jax.numpy as jnp
from jax import lax
from jax.sharding import PartitionSpec as P

QW = 32
KW = 128
REL_CLIP = 4
NREL = 9


def with_halo(block, sides, width):
    for axis, dim in sides:
        count = lax.axis_size(axis)
        forward = [(i, i + 1) for i in range(count - 1)]
        backward = [(target, source) for source, target in forward]
        low = lax.ppermute(
            lax.slice_in_dim(block, block.shape[dim] - width, None, axis=dim), axis, forward
        )
        high = lax.ppermute(lax.slice_in_dim(block, 0, width, axis=dim), axis, backward)
        block = jnp.concatenate([low, block, high], axis=dim)
    return block


def layer_norm(values):
    average = jnp.mean(values, axis=-1, keepdims=True)
    centered = values - average
    variance = jnp.mean(centered * centered, axis=-1, keepdims=True)
    return centered * lax.rsqrt(variance + 1e-05)


def key_windows(padded, window_count, along):
    shifts = KW // QW
    new_shape = padded.shape[:along] + (window_count + shifts - 1, QW) + padded.shape[along + 1 :]
    blocks = padded.reshape(new_shape)
    pieces = [
        lax.slice_in_dim(blocks, start_at, start_at + window_count, axis=along)
        for start_at in range(shifts)
    ]
    stacked = jnp.stack(pieces, axis=along + 1)
    return stacked.reshape(padded.shape[:along] + (window_count, KW) + padded.shape[along + 1 :])


def pair_bias(query_feats, key_feats, key_valid, w_pair_in, w_rel, w_pair_mlp, w_bias):
    highest = lax.Precision.HIGHEST
    differences = query_feats[0:3][:, :, :, None] - key_feats[0:3][:, :, None, :]
    query_tok = query_feats[3][:, :, None]
    key_tok = key_feats[3][:, None, :]
    same_token = jnp.where((query_tok == key_tok) & key_valid[:, None, :], 1.0, 0.0).astype(
        jnp.float32
    )
    inverse = 1.0 / (1.0 + jnp.sum(differences * differences, axis=0))
    token_gap = jnp.clip(key_tok - query_tok, -REL_CLIP, REL_CLIP)
    classes = jnp.arange(NREL, dtype=jnp.float32) - REL_CLIP
    one_hot = jnp.where(token_gap[None] == classes[:, None, None, None], 1.0, 0.0).astype(
        jnp.float32
    )
    pair_rep = (
        jnp.einsum("cx,xwqk->cwqk", w_pair_in[:, 0:3], differences, precision=highest)
        * same_token[None]
    )
    pair_rep = pair_rep + w_pair_in[:, 3][:, None, None, None] * (inverse * same_token)[None]
    pair_rep = pair_rep + w_pair_in[:, 4][:, None, None, None] * same_token[None]
    pair_rep = pair_rep + jnp.einsum("cr,rwqk->cwqk", w_rel, one_hot, precision=highest)
    pair_rep = pair_rep + query_feats[4:][:, :, :, None] + key_feats[4:][:, :, None, :]
    hidden = jax.nn.relu(
        jnp.einsum("dc,cwqk->dwqk", w_pair_mlp[0], jax.nn.relu(pair_rep), precision=highest)
    )
    hidden = jax.nn.relu(jnp.einsum("dc,cwqk->dwqk", w_pair_mlp[1], hidden, precision=highest))
    pair_rep = pair_rep + jnp.einsum("dc,cwqk->dwqk", w_pair_mlp[2], hidden, precision=highest)
    average = jnp.mean(pair_rep, axis=0, keepdims=True)
    centered = pair_rep - average
    variance = jnp.mean(centered * centered, axis=0, keepdims=True)
    normed = centered * lax.rsqrt(jnp.maximum(variance, 0.1))
    return jnp.einsum("lhc,cwqk->lwhqk", w_bias, normed, precision=highest).astype(jnp.bfloat16)


def local(
    atom_act,
    atom_cond,
    ref_pos,
    atom_token,
    w_pair_in,
    w_rel,
    w_cond_pair,
    w_pair_mlp,
    w_bias,
    w_cond,
    w_attn,
    q_bias,
    w_out,
    w_up,
    w_down,
):
    samples, local_atoms, channels = atom_act.shape
    window_count = local_atoms // QW
    head_count = w_bias.shape[1]
    head_dim = channels // head_count
    halo_width = (KW - QW) // 2
    shifts = KW // QW
    hidden_units = w_down.shape[1]
    atom_rank = lax.axis_index("atom")
    total_atoms = local_atoms * lax.axis_size("atom")
    tokens = atom_token.astype(jnp.float32)
    active = jax.nn.relu(atom_cond)
    query_cond = jnp.einsum("ac,cp->pa", active, w_cond_pair[0], preferred_element_type=jnp.float32)
    key_cond = jnp.einsum("ac,cp->pa", active, w_cond_pair[1], preferred_element_type=jnp.float32)
    query_table = jnp.concatenate([ref_pos, tokens[None], query_cond], axis=0)
    key_table = jnp.concatenate([ref_pos, tokens[None], key_cond], axis=0)
    feature_rows = query_table.shape[0]
    key_padded = with_halo(key_table, (("atom", 1),), halo_width)
    position = (
        atom_rank * local_atoms
        - halo_width
        + jnp.arange(window_count)[:, None] * QW
        + jnp.arange(KW)[None, :]
    )
    key_valid = (position >= 0) & (position < total_atoms)
    query_windows = query_table.reshape(feature_rows, window_count, QW)
    share_count = window_count // lax.axis_size("sample")
    first_window = lax.axis_index("sample") * share_count
    my_queries = lax.dynamic_slice_in_dim(query_windows, first_window, share_count, 1)
    key_block = lax.dynamic_slice_in_dim(
        key_padded, first_window * QW, (share_count + shifts - 1) * QW, 1
    )
    my_keys = key_windows(key_block, share_count, 1)
    my_valid = lax.dynamic_slice_in_dim(key_valid, first_window, share_count, 0)
    my_bias = pair_bias(my_queries, my_keys, my_valid, w_pair_in, w_rel, w_pair_mlp, w_bias)
    attn_bias = lax.all_gather(my_bias, "sample", axis=1, tiled=True)
    scale_factor = head_dim ** (-0.5)
    residual = atom_act.astype(jnp.float32)
    for layer_index in range(w_attn.shape[0]):
        cond_values = jnp.dot(atom_cond, w_cond[layer_index], preferred_element_type=jnp.float32)
        modulated = (
            jax.nn.sigmoid(cond_values[:, 0:channels]) * layer_norm(residual)
            + cond_values[:, channels : 2 * channels]
        ).astype(jnp.bfloat16)
        weights = w_attn[layer_index]
        projected = jnp.einsum(
            "sac,cf->saf", modulated, weights, preferred_element_type=jnp.float32
        )
        queries = (projected[..., 0:channels] + q_bias[layer_index]).astype(jnp.bfloat16)
        gating = jax.nn.sigmoid(projected[..., 3 * channels : 4 * channels])
        keyval = projected[..., channels : 3 * channels].astype(jnp.bfloat16)
        keyval_padded = with_halo(keyval, (("atom", 1),), halo_width)
        keyval_windows = key_windows(keyval_padded, window_count, 1)
        query_heads = queries.reshape(samples, window_count, QW, head_count, head_dim)
        key_heads = keyval_windows[..., 0:channels].reshape(
            samples, window_count, KW, head_count, head_dim
        )
        value_heads = keyval_windows[..., channels : 2 * channels].reshape(
            samples, window_count, KW, head_count, head_dim
        )
        scores = (
            jnp.einsum(
                "swqhd,swkhd->swhqk", query_heads, key_heads, preferred_element_type=jnp.float32
            )
            * scale_factor
        )
        scores = scores + attn_bias[layer_index][None].astype(jnp.float32)
        scores = jnp.where(key_valid[None, :, None, None, :], scores, -jnp.inf)
        row_max = jnp.max(scores, axis=-1, keepdims=True)
        exponent = jnp.exp(scores - row_max)
        attn_probs = (exponent / jnp.sum(exponent, axis=-1, keepdims=True)).astype(jnp.bfloat16)
        mixed_out = jnp.einsum(
            "swhqk,swkhd->swqhd", attn_probs, value_heads, preferred_element_type=jnp.float32
        ).reshape(samples, local_atoms, channels)
        mixed_out = (mixed_out * gating).astype(jnp.bfloat16)
        attended = jnp.einsum(
            "sac,cd->sad", mixed_out, w_out[layer_index], preferred_element_type=jnp.float32
        )
        residual = residual + jax.nn.sigmoid(cond_values[:, 2 * channels : 3 * channels]) * attended
        modulated2 = (
            jax.nn.sigmoid(cond_values[:, 3 * channels : 4 * channels]) * layer_norm(residual)
            + cond_values[:, 4 * channels : 5 * channels]
        ).astype(jnp.bfloat16)
        up_values = jnp.einsum(
            "sac,cf->saf", modulated2, w_up[layer_index], preferred_element_type=jnp.float32
        )
        hidden = (
            jax.nn.silu(up_values[..., 0:hidden_units])
            * up_values[..., hidden_units : 2 * hidden_units]
        ).astype(jnp.bfloat16)
        transition = jnp.einsum(
            "saf,fc->sac", hidden, w_down[layer_index], preferred_element_type=jnp.float32
        )
        residual = (
            residual + jax.nn.sigmoid(cond_values[:, 5 * channels : 6 * channels]) * transition
        )
    return residual.astype(jnp.bfloat16)


def solution(mesh):
    in_specs = (
        P("sample", "atom", None),
        P("atom", None),
        P(None, "atom"),
        P("atom"),
        P(),
        P(),
        P(),
        P(),
        P(),
        P(),
        P(),
        P(),
        P(),
        P(),
        P(),
    )
    out_specs = P("sample", "atom", None)
    return jax.shard_map(local, mesh=mesh, in_specs=in_specs, out_specs=out_specs, check_vma=False)
```

profile of v0, /device:TPU:30, one launch (start us, length us, event | category | flops | bytes accessed | tf_op | source)
XLA Modules:
  0.0 158.6 jit_solution(17236440815866380441)
XLA Ops:
  3.4 1.2 fusion.242
  5.3 7.8 %collective-permute-start.1 = (bf16[2,48,256]{2,1,0:T(8,128)(2,1)}, bf16[2,48,256]{2,1,0:T(8,128)(2,1)}, u32[]{:S(2)}, u32[]{:S(2)}) collective-permute-start(bf16[2,48,256]{2,1,0:T(8,128)(2,1)} %get-tuple-element.37), channel_id=1, source_target_pairs={{8,0},{16,8},{24,16},{32,24},{40,32},{48,40},{56,48},{64,56},{72,6... | collective-permute-start | bytes 147464 | tf_op jit(solution)/shard_map/ppermute | solution.py:20
  13.1 1.9 %collective-permute-start = (bf16[2,48,256]{2,1,0:T(8,128)(2,1)}, bf16[2,48,256]{2,1,0:T(8,128)(2,1)}, u32[]{:S(2)}, u32[]{:S(2)}) collective-permute-start(bf16[2,48,256]{2,1,0:T(8,128)(2,1)} %get-tuple-element.36), channel_id=1, source_target_pairs={{0,8},{8,16},{16,24},{24,32},{32,40},{40,48},{48,56},{56,64},{64,7... | collective-permute-start | bytes 147464 | tf_op jit(solution)/shard_map/ppermute | solution.py:17
  16.4 1.9 %collective-permute-start.2 = (f32[20,48]{1,0:T(8,128)}, f32[20,48]{1,0:T(8,128)S(1)}, u32[]{:S(2)}, u32[]{:S(2)}) collective-permute-start(f32[20,48]{1,0:T(8,128)} %get-tuple-element.55), channel_id=1, source_target_pairs={{0,8},{8,16},{16,24},{24,32},{32,40},{40,48},{48,56},{56,64},{64,7... | collective-permute-start | bytes 11528 | tf_op jit(solution)/shard_map/ppermute | solution.py:17
  18.3 6.7 %collective-permute-start.3 = (f32[20,48]{1,0:T(8,128)}, f32[20,48]{1,0:T(8,128)}, u32[]{:S(2)}, u32[]{:S(2)}) collective-permute-start(f32[20,48]{1,0:T(8,128)} %get-tuple-element.54), channel_id=1, source_target_pairs={{8,0},{16,8},{24,16},{32,24},{40,32},{48,40},{56,48},{64,56},{72,6... | collective-permute-start | bytes 11528 | tf_op jit(solution)/shard_map/ppermute | solution.py:20
  29.6 1.3 slice_bitcast_fusion.23
  55.6 29.9 %all_gather.3 = bf16[3,8,4,32,128]{4,3,2,0,1:T(8,128)(2,1)S(1)} all-gather(bf16[3,1,4,32,128]{4,3,2,0,1:T(8,128)(2,1)S(1)} %copy.198), channel_id=1, replica_groups=mesh['atom'=32,'sample'=8] {'sample'}, dimensions={1}, use_global_device_ids=true | all-gather | bytes 884736 | tf_op jit(solution)/shard_map/all_gather | solution.py:129
  89.4 1.3 fusion.14
  91.7 4.6 %convolution_bitcast_fusion.2 = f32[2,8,32,4,32]{2,4,3,1,0:T(8,128)} fusion(bf16[2,8,128,4,32]{2,4,3,1,0:T(8,128)(2,1)S(1)} %bitcast.277, f32[2,8,4,32]{3,2,1,0:T(4,128)S(1)} %fusion.244, f32[2,8,4,32,128]{4,3,2,1,0:T(8,128)S(1)} %fusion.14), kind=kOutput, calls=%fused_computation.17 | convolution fusion | flops 17565824 | bytes 1843200 | tf_op jit(solution)/shard_map/swhqk,swkhd->swqhd/dot_general | solution.py:165
  96.4 1.6 %copy.199 = f32[2,8,32,4,32]{4,3,2,1,0:T(4,128)S(1)} copy(f32[2,8,32,4,32]{2,4,3,1,0:T(8,128)} %convolution_bitcast_fusion.2) | data formatting | bytes 524288 | tf_op jit(solution)/shard_map/swhqk,swkhd->swqhd/transpose | solution.py:165
  101.1 1.3 fusion.89
  104.5 1.2 fusion.247
  105.8 1.9 %collective-permute-start.5 = (bf16[2,48,256]{2,1,0:T(8,128)(2,1)S(1)}, bf16[2,48,256]{2,1,0:T(8,128)(2,1)S(1)}, u32[]{:S(2)}, u32[]{:S(2)}) collective-permute-start(bf16[2,48,256]{2,1,0:T(8,128)(2,1)S(1)} %get-tuple-element.35), channel_id=1, source_target_pairs={{8,0},{16,8},{24,16},{32,24},{40,32},{48,40},{56,48},{64,56},{72,6... | collective-permute-start | bytes 147464 | tf_op jit(solution)/shard_map/ppermute | solution.py:20
  107.7 2.6 %collective-permute-start.4 = (bf16[2,48,256]{2,1,0:T(8,128)(2,1)S(1)}, bf16[2,48,256]{2,1,0:T(8,128)(2,1)S(1)}, u32[]{:S(2)}, u32[]{:S(2)}) collective-permute-start(bf16[2,48,256]{2,1,0:T(8,128)(2,1)S(1)} %get-tuple-element.34), channel_id=1, source_target_pairs={{0,8},{8,16},{16,24},{24,32},{32,40},{40,48},{48,56},{56,64},{64,7... | collective-permute-start | bytes 147464 | tf_op jit(solution)/shard_map/ppermute | solution.py:17
  111.2 5.0 %collective-permute-done.4 = bf16[2,48,256]{2,1,0:T(8,128)(2,1)S(1)} collective-permute-done((bf16[2,48,256]{2,1,0:T(8,128)(2,1)S(1)}, bf16[2,48,256]{2,1,0:T(8,128)(2,1)S(1)}, u32[]{:S(2)}, u32[]{:S(2)}) %collective-permute-start.4) | collective-permute-done | bytes 49184 | tf_op jit(solution)/shard_map/ppermute | solution.py:17
  119.5 4.6 %convolution_bitcast_fusion.1 = f32[2,8,32,4,32]{2,4,3,1,0:T(8,128)} fusion(bf16[2,8,128,4,32]{2,4,3,1,0:T(8,128)(2,1)S(1)} %bitcast.278, f32[2,8,4,32]{3,2,1,0:T(4,128)S(1)} %fusion.248, f32[2,8,4,32,128]{4,3,2,1,0:T(8,128)S(1)} %fusion.12), kind=kOutput, calls=%fused_computation.13 | convolution fusion | flops 17565824 | bytes 1843200 | tf_op jit(solution)/shard_map/swhqk,swkhd->swqhd/dot_general | solution.py:165
  124.1 1.6 %copy.216 = f32[2,8,32,4,32]{4,3,2,1,0:T(4,128)S(1)} copy(f32[2,8,32,4,32]{2,4,3,1,0:T(8,128)} %convolution_bitcast_fusion.1) | data formatting | bytes 524288 | tf_op jit(solution)/shard_map/swhqk,swkhd->swqhd/transpose | solution.py:165
  128.8 1.3 fusion.91
  133.5 1.9 %collective-permute-start.7 = (bf16[2,48,256]{2,1,0:T(8,128)(2,1)S(1)}, bf16[2,48,256]{2,1,0:T(8,128)(2,1)S(1)}, u32[]{:S(2)}, u32[]{:S(2)}) collective-permute-start(bf16[2,48,256]{2,1,0:T(8,128)(2,1)S(1)} %get-tuple-element.33), channel_id=1, source_target_pairs={{8,0},{16,8},{24,16},{32,24},{40,32},{48,40},{56,48},{64,56},{72,6... | collective-permute-start | bytes 147464 | tf_op jit(solution)/shard_map/ppermute | solution.py:20
  135.5 2.4 %collective-permute-start.6 = (bf16[2,48,256]{2,1,0:T(8,128)(2,1)S(1)}, bf16[2,48,256]{2,1,0:T(8,128)(2,1)S(1)}, u32[]{:S(2)}, u32[]{:S(2)}) collective-permute-start(bf16[2,48,256]{2,1,0:T(8,128)(2,1)S(1)} %get-tuple-element.32), channel_id=1, source_target_pairs={{0,8},{8,16},{16,24},{24,32},{32,40},{40,48},{48,56},{56,64},{64,7... | collective-permute-start | bytes 147464 | tf_op jit(solution)/shard_map/ppermute | solution.py:17
  138.8 5.1 %collective-permute-done.6 = bf16[2,48,256]{2,1,0:T(8,128)(2,1)S(1)} collective-permute-done((bf16[2,48,256]{2,1,0:T(8,128)(2,1)S(1)}, bf16[2,48,256]{2,1,0:T(8,128)(2,1)S(1)}, u32[]{:S(2)}, u32[]{:S(2)}) %collective-permute-start.6) | collective-permute-done | bytes 49184 | tf_op jit(solution)/shard_map/ppermute | solution.py:17
  146.0 4.6 %convolution_bitcast_fusion = f32[2,8,32,4,32]{2,4,3,1,0:T(8,128)} fusion(bf16[2,8,128,4,32]{2,4,3,1,0:T(8,128)(2,1)S(1)} %bitcast.276, f32[2,8,4,32]{3,2,1,0:T(4,128)S(1)} %fusion.252, f32[2,8,4,32,128]{4,3,2,1,0:T(8,128)S(1)} %fusion.10), kind=kOutput, calls=%fused_computation.9 | convolution fusion | flops 17565824 | bytes 1843200 | tf_op jit(solution)/shard_map/swhqk,swkhd->swqhd/dot_general | solution.py:165
  150.6 1.6 %copy.233 = f32[2,8,32,4,32]{4,3,2,1,0:T(4,128)S(1)} copy(f32[2,8,32,4,32]{2,4,3,1,0:T(8,128)} %convolution_bitcast_fusion) | data formatting | bytes 524288 | tf_op jit(solution)/shard_map/swhqk,swkhd->swqhd/transpose | solution.py:165
  155.4 1.3 fusion.93
  (238 shorter events, 62.8 us)
Async XLA Ops:
  0.0 51.9 %copy-start = (f32[16,9]{1,0:T(8,128)S(1)}, f32[16,9]{1,0:T(8,128)}, u32[]{:S(2)}) copy-start(f32[16,9]{1,0:T(8,128)} %param.20) | copy-start | bytes 1732
  0.0 1.0 copy-start.1
  4.6 28.0 %copy-start.2 = (f32[2,256,512]{2,1,0:T(8,128)}, f32[2,256,512]{2,1,0:T(8,128)S(1)}, u32[]{:S(2)}) copy-start(f32[2,256,512]{2,1,0:T(8,128)S(1)} %get-tuple-element.65) | copy-start | bytes 3145732
  4.6 10.4 %copy-start.37 = (bf16[2,128,16]{1,2,0:T(8,128)(2,1)S(1)}, bf16[2,128,16]{1,2,0:T(8,128)(2,1)}, u32[]{:S(2)}) copy-start(bf16[2,128,16]{1,2,0:T(8,128)(2,1)} %param.21) | copy-start | bytes 24580
  5.3 81.3 %collective-permute-start.1 = (bf16[2,48,256]{2,1,0:T(8,128)(2,1)}, bf16[2,48,256]{2,1,0:T(8,128)(2,1)}, u32[]{:S(2)}, u32[]{:S(2)}) collective-permute-start(bf16[2,48,256]{2,1,0:T(8,128)(2,1)} %get-tuple-element.37), channel_id=1, source_target_pairs={{8,0},{16,8},{24,16},{32,24},{40,32},{48,40},{56,48},{64,56},{72,6... | collective-permute-start | bytes 147464 | tf_op jit(solution)/shard_map/ppermute | solution.py:20
  13.1 2.1 %copy-start.43 = (s32[256]{0:T(256)S(1)}, s32[256]{0:T(256)}, u32[]{:S(2)}) copy-start(s32[256]{0:T(256)} %param.18) | copy-start | bytes 3076
  13.1 73.5 %collective-permute-start = (bf16[2,48,256]{2,1,0:T(8,128)(2,1)}, bf16[2,48,256]{2,1,0:T(8,128)(2,1)}, u32[]{:S(2)}, u32[]{:S(2)}) collective-permute-start(bf16[2,48,256]{2,1,0:T(8,128)(2,1)} %get-tuple-element.36), channel_id=1, source_target_pairs={{0,8},{8,16},{16,24},{24,32},{32,40},{40,48},{48,56},{56,64},{64,7... | collective-permute-start | bytes 147464 | tf_op jit(solution)/shard_map/ppermute | solution.py:17
  16.4 32.2 %collective-permute-start.2 = (f32[20,48]{1,0:T(8,128)}, f32[20,48]{1,0:T(8,128)S(1)}, u32[]{:S(2)}, u32[]{:S(2)}) collective-permute-start(f32[20,48]{1,0:T(8,128)} %get-tuple-element.55), channel_id=1, source_target_pairs={{0,8},{8,16},{16,24},{24,32},{32,40},{40,48},{48,56},{56,64},{64,7... | collective-permute-start | bytes 11528 | tf_op jit(solution)/shard_map/ppermute | solution.py:17
  18.3 30.3 %collective-permute-start.3 = (f32[20,48]{1,0:T(8,128)}, f32[20,48]{1,0:T(8,128)}, u32[]{:S(2)}, u32[]{:S(2)}) collective-permute-start(f32[20,48]{1,0:T(8,128)} %get-tuple-element.54), channel_id=1, source_target_pairs={{8,0},{16,8},{24,16},{32,24},{40,32},{48,40},{56,48},{64,56},{72,6... | collective-permute-start | bytes 11528 | tf_op jit(solution)/shard_map/ppermute | solution.py:20
  27.0 1.2 copy-start.42
  29.0 4.4 %copy-start.34 = (f32[20,1,32]{2,1,0:T(1,128)}, f32[20,1,32]{2,1,0:T(1,128)S(1)}, u32[]{:S(2)}) copy-start(f32[20,1,32]{2,1,0:T(1,128)S(1)} %fusion.202) | copy-start | bytes 7684
  33.4 1.7 %copy-start.11 = (f32[256,128]{1,0:T(8,128)S(1)}, f32[256,128]{1,0:T(8,128)}, u32[]{:S(2)}) copy-start(f32[256,128]{1,0:T(8,128)} %get-tuple-element.31) | copy-start | bytes 393220
  90.7 1.0 copy-start.20
  100.1 1.0 copy-start.27
  101.1 1.3 copy-start.32
  105.8 5.2 %copy-start.4 = (f32[2,256,512]{2,1,0:T(8,128)}, f32[2,256,512]{2,1,0:T(8,128)S(1)}, u32[]{:S(2)}) copy-start(f32[2,256,512]{2,1,0:T(8,128)S(1)} %get-tuple-element.73) | copy-start | bytes 3145732
  105.8 5.4 %collective-permute-start.5 = (bf16[2,48,256]{2,1,0:T(8,128)(2,1)S(1)}, bf16[2,48,256]{2,1,0:T(8,128)(2,1)S(1)}, u32[]{:S(2)}, u32[]{:S(2)}) collective-permute-start(bf16[2,48,256]{2,1,0:T(8,128)(2,1)S(1)} %get-tuple-element.35), channel_id=1, source_target_pairs={{8,0},{16,8},{24,16},{32,24},{40,32},{48,40},{56,48},{64,56},{72,6... | collective-permute-start | bytes 147464 | tf_op jit(solution)/shard_map/ppermute | solution.py:20
  107.7 8.5 %collective-permute-start.4 = (bf16[2,48,256]{2,1,0:T(8,128)(2,1)S(1)}, bf16[2,48,256]{2,1,0:T(8,128)(2,1)S(1)}, u32[]{:S(2)}, u32[]{:S(2)}) collective-permute-start(bf16[2,48,256]{2,1,0:T(8,128)(2,1)S(1)} %get-tuple-element.34), channel_id=1, source_target_pairs={{0,8},{8,16},{16,24},{24,32},{32,40},{40,48},{48,56},{56,64},{64,7... | collective-permute-start | bytes 147464 | tf_op jit(solution)/shard_map/ppermute | solution.py:17
  118.5 1.0 copy-start.21
  128.8 1.3 copy-start.30
  133.5 5.0 %copy-start.3 = (f32[2,256,512]{2,1,0:T(8,128)}, f32[2,256,512]{2,1,0:T(8,128)S(1)}, u32[]{:S(2)}) copy-start(f32[2,256,512]{2,1,0:T(8,128)S(1)} %get-tuple-element.79) | copy-start | bytes 3145732
  133.5 5.3 %collective-permute-start.7 = (bf16[2,48,256]{2,1,0:T(8,128)(2,1)S(1)}, bf16[2,48,256]{2,1,0:T(8,128)(2,1)S(1)}, u32[]{:S(2)}, u32[]{:S(2)}) collective-permute-start(bf16[2,48,256]{2,1,0:T(8,128)(2,1)S(1)} %get-tuple-element.33), channel_id=1, source_target_pairs={{8,0},{16,8},{24,16},{32,24},{40,32},{48,40},{56,48},{64,56},{72,6... | collective-permute-start | bytes 147464 | tf_op jit(solution)/shard_map/ppermute | solution.py:20
  135.5 8.4 %collective-permute-start.6 = (bf16[2,48,256]{2,1,0:T(8,128)(2,1)S(1)}, bf16[2,48,256]{2,1,0:T(8,128)(2,1)S(1)}, u32[]{:S(2)}, u32[]{:S(2)}) collective-permute-start(bf16[2,48,256]{2,1,0:T(8,128)(2,1)S(1)} %get-tuple-element.32), channel_id=1, source_target_pairs={{0,8},{8,16},{16,24},{24,32},{32,40},{40,48},{48,56},{56,64},{64,7... | collective-permute-start | bytes 147464 | tf_op jit(solution)/shard_map/ppermute | solution.py:17
  155.4 1.3 copy-start.28
  (35 other events, 28.8 us)
where the time goes:
time: 160 us; the launch traced here: 159 us
  local copies, waits for them, and re-layouts  44.7 us (28%)
  matrix products  36.6 us (23%)
  blocking collectives  29.9 us (19%)
  starting transfers between devices  27.1 us (17%)
  waiting for transfers between devices  10.1 us (6%)
  other arithmetic  9.14 us (6%)
    all_gather x1, blocking collectives, local(): attn_bias = lax.all_gather(my_bias, 'sample', axis=1, tiled=True)  29.9 us
    ppermute x4, starting transfers between devices, with_halo(): lax.ppermute(lax.slice_in_dim(block, 0, width, axis=dim), axis, backward)  18.3 us
    unnamed x100, local copies, waits for them, and re-layouts  14.4 us
    dot_general x3, matrix products, local(): jnp.einsum('swhqk,swkhd->swqhd', attn_probs, value_heads, preferred_eleme...  13.9 us
    ppermute x4, waiting for transfers between devices, with_halo(): lax.ppermute(lax.slice_in_dim(block, block.shape[dim] - width, None, axis...  10 us
    ppermute x4, starting transfers between devices, with_halo(): lax.ppermute(lax.slice_in_dim(block, block.shape[dim] - width, None, axis...  8.82 us
    div x12, local copies, waits for them, and re-layouts, local(): jax.nn.sigmoid(cond_values[:, 0:channels]) * layer_norm(residual)  8.4 us
    transpose x3, local copies, waits for them, and re-layouts, local(): jnp.einsum('swhqk,swkhd->swqhd', attn_probs, value_heads, preferred_eleme...  4.88 us
  transfers between devices with their start and end apart: 8, of which 2 were waited for; matrix products, arithmetic and copies ran while one was open for 17% of the time, Pallas kernels for 0%

commit v1 on v0

v1 whole, which is shorter than its diff:
```python
import functools

import jax
import jax.numpy as jnp
from jax import lax
from jax.experimental import pallas as pl
from jax.experimental.pallas import tpu as pltpu
from jax.sharding import PartitionSpec as P

F32 = jnp.float32
BF16 = jnp.bfloat16
MESH = pl.DeviceIdType.MESH

S = 2
A = 256
C = 128
HEADS = 4
HD = 32
FFH = 256
CP = 16
QW = 32
HALO = 48
LAYERS = 3
EXT = A + 2 * HALO
LOG2E = 1.4426950408889634
SCALE = HD**-0.5
NEG = -1e30
WINDOWS = ((0, 1, 6, 7), (2, 3, 4, 5))
SEGMENTS = (((0, 0, 64), (64, 192, 64)), ((0, 64, 128),))


def dot(a, b):
    return lax.dot_general(a, b, (((1,), (0,)), ((), ())), preferred_element_type=F32)


def dot_nt(a, b):
    return lax.dot_general(a, b, (((1,), (1,)), ((), ())), preferred_element_type=F32)


def sigmoid(x):
    return 0.5 * jnp.tanh(0.5 * x) + 0.5


def layer_norm(x):
    mean = jnp.mean(x, axis=-1, keepdims=True)
    xc = x - mean
    var = jnp.mean(xc * xc, axis=-1, keepdims=True)
    return xc * lax.rsqrt(var + 1e-05)


def iota(shape, dim):
    return lax.broadcasted_iota(jnp.int32, shape, dim)


def spread(rows, cols):
    return jnp.where(iota((rows, cols), 0) // 16 == iota((rows, cols), 1), 1.0, 0.0).astype(BF16)


def kron16(m, e_rows, e_cols):
    wide = dot(e_rows, m.astype(BF16)).astype(BF16)
    full = dot_nt(wide, e_cols)
    same = iota(full.shape, 0) % 16 == iota(full.shape, 1) % 16
    return jnp.where(same, full, 0.0)


def kernel(
    act_h, cond_h, pos_h, tok_h, wpi_h, wrel_h, wcp_h, wmlp_h, wb_h, wcond_h, wattn_h, qb_h,
    wout_h, wup_h, wdown_h, out_ref,
    act, cext, t3, tk, wpi, wrel, wcp, wmlp, wb, wcond, wattn, qb, wout, wup, wdown,
    cv, res, qs, gs, mix, kv, bias, emb, cm, km, wbk, qt, qcp, kt, kc,
    lsem, ssem, rsem,
):
    atom = lax.axis_index("atom")
    natom = lax.axis_size("atom")
    right = lax.rem(atom + 1, natom)
    left = lax.rem(atom + natom - 1, natom)

    barrier = pltpu.get_barrier_semaphore()
    for nb in (left, right):
        pl.semaphore_signal(barrier, inc=1, device_id={"atom": nb}, device_id_type=MESH)

    local = []
    for i, (src, dst) in enumerate(
        (
            (act_h, act),
            (cond_h, cext.at[HALO : HALO + A]),
            (wcond_h.at[0], wcond.at[0]),
            (wattn_h, wattn),
            (qb_h, qb),
            (pos_h, t3.at[:, A : 2 * A]),
            (tok_h, tk.at[:, A : 2 * A]),
            (wpi_h, wpi),
            (wrel_h, wrel),
            (wcp_h, wcp),
            (wmlp_h, wmlp),
            (wb_h, wb),
            (wcond_h.at[1:3], wcond.at[1:3]),
            (wout_h, wout),
            (wup_h, wup),
            (wdown_h, wdown),
        )
    ):
        copy = pltpu.make_async_copy(src, dst, lsem.at[i])
        copy.start()
        local.append(copy)

    remote = []

    def send(src, dst, index, to):
        copy = pltpu.make_async_remote_copy(
            src_ref=src,
            dst_ref=dst,
            send_sem=ssem.at[index],
            recv_sem=rsem.at[index],
            device_id={"atom": to},
            device_id_type=MESH,
        )
        copy.start()
        remote.append(copy)

    def send_kv(layer):
        send(kv.at[layer, :, A : A + HALO], kv.at[layer, :, 0:HALO], 2 * layer, right)
        send(kv.at[layer, :, HALO : 2 * HALO], kv.at[layer, :, HALO + A : EXT], 2 * layer + 1, left)

    def cond_rows(group):
        return [cext[HALO + a0 : HALO + a0 + n] for _, a0, n in SEGMENTS[group]]

    def cond_values(layer):
        cond = jnp.concatenate(cond_rows(0) + cond_rows(1), axis=0)
        for part in range(6):
            vals = dot(cond, wcond[layer, :, part * C : (part + 1) * C])
            cv[layer, part] = vals if part in (1, 4) else sigmoid(vals)

    def project(layer, group):
        rows = slice(group * 128, group * 128 + 128)
        mods = []
        for s in range(S):
            mods.append(
                (cv[layer, 0, rows] * layer_norm(res[group, s]) + cv[layer, 1, rows]).astype(BF16)
            )
        mod = jnp.concatenate(mods, axis=0)
        q = dot(mod, wattn[layer, :, 0:C]) + qb[layer : layer + 1, :]
        qs[group] = q.astype(BF16).reshape(S, 128, C)
        keyval = dot(mod, wattn[layer, :, C : 3 * C]).astype(BF16)
        for s in range(S):
            for r0, a0, n in SEGMENTS[group]:
                kv[layer, s, HALO + a0 : HALO + a0 + n] = keyval[s * 128 + r0 : s * 128 + r0 + n]
        gate = dot(mod, wattn[layer, :, 3 * C : 4 * C])
        gs[group] = sigmoid(gate).reshape(S, 128, C)

    lane = iota((QW, C), 1)
    head_masks = [jnp.where(lane // HD == h, 1.0, 0.0).astype(BF16) for h in range(HEADS)]
    ones = jnp.ones((C, C), BF16)

    def by_head(x, c0):
        parts = [x[h * QW : (h + 1) * QW, c0 : c0 + C] for h in range(HEADS)]
        out = parts[HEADS - 1]
        for h in range(HEADS - 2, -1, -1):
            out = jnp.where(lane < (h + 1) * HD, parts[h], out)
        return out

    def attend(layer, group):
        for j in range(4):
            w = WINDOWS[group][j]
            for s in range(S):
                q = qs[group, s, j * QW : (j + 1) * QW]
                big = jnp.concatenate([q * m for m in head_masks], axis=0)
                k = kv[layer, s, w * QW : w * QW + C, 0:C]
                v = kv[layer, s, w * QW : w * QW + C, C : 2 * C]
                t = dot_nt(big, k) * (SCALE * LOG2E) + bias[layer, group, j]
                top = jnp.max(t, axis=-1, keepdims=True)
                e = jnp.exp2(t - top).astype(BF16)
                o = dot(e, jnp.concatenate([v, ones], axis=1))
                mixed = by_head(o, 0) / by_head(o, C) * gs[group, s, j * QW : (j + 1) * QW]
                mix[group, s, j * QW : (j + 1) * QW] = mixed.astype(BF16)

    def transition(layer, group):
        rows = slice(group * 128, group * 128 + 128)
        attended = dot(mix[group].reshape(S * 128, C), wout[layer])
        mods = []
        for s in range(S):
            r = res[group, s] + cv[layer, 2, rows] * attended[s * 128 : (s + 1) * 128]
            res[group, s] = r
            mods.append((cv[layer, 3, rows] * layer_norm(r) + cv[layer, 4, rows]).astype(BF16))
        mod = jnp.concatenate(mods, axis=0)
        up = dot(mod, wup[layer, :, 0:FFH])
        hidden = (up * sigmoid(up) * dot(mod, wup[layer, :, FFH : 2 * FFH])).astype(BF16)
        down = dot(hidden, wdown[layer])
        for s in range(S):
            r = res[group, s] + cv[layer, 5, rows] * down[s * 128 : (s + 1) * 128]
            if layer < LAYERS - 1:
                res[group, s] = r
            else:
                for r0, a0, n in SEGMENTS[group]:
                    out_ref[s, a0 : a0 + n] = r[r0 : r0 + n].astype(BF16)

    def pair_constants():
        e16 = spread(256, 16)
        r16 = iota((16, 16), 0)
        c16 = iota((16, 16), 1)
        place = jnp.where(c16 == jnp.where(r16 < 4, r16, 8), 1.0, 0.0)
        shift = jnp.where(c16 == r16 + 4, 1.0, 0.0)
        weights = lax.dot_general(
            wpi[...], place[0:5], (((1,), (0,)), ((), ())),
            precision=lax.Precision.HIGHEST, preferred_element_type=F32,
        ) + lax.dot_general(
            wrel[...], shift[0:9], (((1,), (0,)), ((), ())),
            precision=lax.Precision.HIGHEST, preferred_element_type=F32,
        )
        base = kron16(weights, e16, e16)
        row = iota((256, 256), 0)
        col = iota((256, 256), 1)
        keyed = (col >= 208) & (col < 240) & (row // 16 == col % 16)
        emb[...] = jnp.where(keyed, 1.0, jnp.where(col < 208, base, 0.0)).astype(BF16)
        cm[...] = jnp.where(
            iota((256, C), 1) == 112 + iota((256, C), 0) // 16, 1.0, 0.0
        ).astype(BF16)
        for i in range(3):
            km[i] = kron16(wmlp[i], e16, e16).astype(BF16)
        e4 = spread(64, HEADS)
        for layer in range(LAYERS):
            wbk[layer * 64 : (layer + 1) * 64] = kron16(wb[layer], e4, e16).astype(BF16)

    def query_tables():
        pos = jnp.concatenate(
            [t3[:, A : 2 * A], tk[:, A : 2 * A].astype(F32), jnp.zeros((124, A), F32)], axis=0
        )
        cols = pos.T
        off = 0
        for group in range(2):
            for _, a0, n in SEGMENTS[group]:
                qt[off : off + n] = cols[a0 : a0 + n]
                off += n
        place = jnp.where(iota((16, C), 1) == 112 + iota((16, C), 0), 1.0, 0.0).astype(BF16)
        w0 = dot(wcp[0], place).astype(BF16)
        cond = jnp.concatenate(cond_rows(0) + cond_rows(1), axis=0)
        qcp[...] = dot(jnp.maximum(cond, 0), w0).astype(BF16)

    def key_tables(group):
        eye = jnp.where(iota((16, 16), 0) == iota((16, 16), 1), 1.0, 0.0).astype(BF16)
        w1 = dot_nt(eye, wcp[1]).astype(BF16)
        for j in range(4):
            w = WINDOWS[group][j]
            cond = jnp.maximum(cext[w * QW : w * QW + C], 0)
            full = dot_nt(w1, cond)
            hi = full.astype(BF16)
            kc[group, j, 0:16] = hi
            kc[group, j, 16:32] = (full - hi.astype(F32)).astype(BF16)
            first = A - HALO + w * QW
            a0 = first // 128 * 128
            wide = jnp.concatenate(
                [t3[:, a0 : a0 + 256], tk[:, a0 : a0 + 256].astype(F32), jnp.zeros((4, 256), F32)],
                axis=0,
            )
            if first > a0:
                wide = pltpu.roll(wide, 256 - (first - a0), 1)
            kt[group, j] = wide[:, 0:C]

    def bias_unit(group, jp, half):
        feats = []
        for i in range(2):
            j = 2 * jp + i
            q0 = pl.multiple_of(group * 128 + j * QW + half * 16, 16)
            qcols = qt[pl.ds(q0, 16), :]
            keys = kt[group, j]
            d = [qcols[:, x : x + 1] - keys[x : x + 1, :] for x in range(3)]
            inv = 1.0 / (1.0 + (d[0] * d[0] + d[1] * d[1] + d[2] * d[2]))
            gap = jnp.clip(keys[3:4, :] - qcols[:, 3:4], -4.0, 4.0)
            hot = [jnp.where(gap == float(g), 1.0, 0.0) for g in range(-4, 5)]
            v = hot[4]
            rows = [v * x for x in d] + [v * inv] + hot
            rhs = jnp.concatenate(
                [x.astype(BF16) for x in rows] + [kc[group, j], jnp.ones((16, C), BF16)], axis=0
            )
            qc = qcp[pl.ds(q0, 16), :]
            tail = emb[:, C : 2 * C] + cm[...] * jnp.concatenate([qc] * 16, axis=0)
            lhs = jnp.concatenate([emb[:, 0:C], tail], axis=1)
            feats.append(dot(lhs, rhs))
        pair = jnp.concatenate(feats, axis=1)
        h = jnp.maximum(dot(km[0], jnp.maximum(pair, 0.0).astype(BF16)), 0.0).astype(BF16)
        h = jnp.maximum(dot(km[1], h), 0.0).astype(BF16)
        pair = (pair + dot(km[2], h)).reshape(CP, 16, 256)
        mean = jnp.sum(pair, axis=0) * (1.0 / CP)
        centered = pair - mean[None]
        var = jnp.sum(centered * centered, axis=0) * (1.0 / CP)
        normed = (centered * lax.rsqrt(jnp.maximum(var, 0.1))[None]).astype(BF16)
        out = dot(wbk[...], normed.reshape(256, 256))
        for i in range(2):
            j = 2 * jp + i
            w = jnp.where(group == 0, jnp.where(j < 2, j, j + 4), j + 2)
            at = atom * A + w * QW - HALO + iota((1, C), 1)
            mask = jnp.where((at >= 0) & (at < natom * A), 0.0, NEG)
            part = out[:, i * C : (i + 1) * C].astype(BF16).astype(F32) * LOG2E + mask
            for layer in range(LAYERS):
                for h in range(HEADS):
                    r0 = layer * 64 + h * 16
                    bias[layer, group, j, pl.ds(h * QW + half * 16, 16), :] = part[r0 : r0 + 16]

    def pair_bias(group):
        @pl.loop(0, 2)
        def _(jp):
            for half in range(2):
                bias_unit(group, jp, half)

    def wait(*which):
        for i in which:
            local[i].wait()

    wait(0, 1, 2, 3, 4)
    for group in range(2):
        for s in range(S):
            for r0, a0, n in SEGMENTS[group]:
                res[group, s, r0 : r0 + n] = act[s, a0 : a0 + n].astype(F32)
    cond_values(0)
    project(0, 0)
    pl.semaphore_wait(barrier, 2)
    send(cond_h.at[A - HALO : A], cext.at[0:HALO], 6, right)
    send(cond_h.at[0:HALO], cext.at[HALO + A : EXT], 7, left)
    send(pos_h, t3.at[:, 0:A], 8, right)
    send(pos_h, t3.at[:, 2 * A : 3 * A], 9, left)
    send(tok_h, tk.at[:, 0:A], 10, right)
    send(tok_h, tk.at[:, 2 * A : 3 * A], 11, left)
    send_kv(0)
    project(0, 1)
    wait(5, 6, 7, 8, 9, 10, 11)
    pair_constants()
    query_tables()
    key_tables(1)
    pair_bias(1)
    wait(12, 13, 14, 15)
    cond_values(1)
    cond_values(2)
    attend(0, 1)
    transition(0, 1)
    project(1, 1)

    for copy in remote[0:6]:
        copy.wait_recv()
    key_tables(0)
    pair_bias(0)
    for copy in remote[6:8]:
        copy.wait_recv()
    attend(0, 0)
    transition(0, 0)
    project(1, 0)
    send_kv(1)
    for layer in (1, 2):
        attend(layer, 1)
        transition(layer, 1)
        if layer == 1:
            project(2, 1)
        for copy in remote[6 + 2 * layer : 8 + 2 * layer]:
            copy.wait_recv()
        attend(layer, 0)
        transition(layer, 0)
        if layer == 1:
            project(2, 0)
            send_kv(2)
    for copy in remote:
        copy.wait_send()


def local(*args):
    args = list(args)
    args[3] = args[3].reshape(1, A)
    vmem = pltpu.VMEM
    return pl.pallas_call(
        kernel,
        out_shape=jax.ShapeDtypeStruct((S, A, C), BF16),
        in_specs=[pl.BlockSpec(memory_space=pl.ANY)] * 15,
        out_specs=pl.BlockSpec(memory_space=pltpu.VMEM),
        scratch_shapes=[
            vmem((S, A, C), BF16),
            vmem((EXT, C), BF16),
            vmem((3, 3 * A), F32),
            vmem((1, 3 * A), jnp.int32),
            vmem((CP, 5), F32),
            vmem((CP, 9), F32),
            vmem((2, C, CP), BF16),
            vmem((3, CP, CP), F32),
            vmem((LAYERS, HEADS, CP), F32),
            vmem((LAYERS, C, 6 * C), BF16),
            vmem((LAYERS, C, 4 * C), BF16),
            vmem((LAYERS, C), F32),
            vmem((LAYERS, C, C), BF16),
            vmem((LAYERS, C, 2 * FFH), BF16),
            vmem((LAYERS, FFH, C), BF16),
            vmem((LAYERS, 6, A, C), F32),
            vmem((2, S, 128, C), F32),
            vmem((2, S, 128, C), BF16),
            vmem((2, S, 128, C), F32),
            vmem((2, S, 128, C), BF16),
            vmem((LAYERS, S, EXT, 2 * C), BF16),
            vmem((LAYERS, 2, 4, HEADS * QW, C), F32),
            vmem((256, 256), BF16),
            vmem((256, C), BF16),
            vmem((3, 256, 256), BF16),
            vmem((192, 256), BF16),
            vmem((A, C), F32),
            vmem((A, C), BF16),
            vmem((2, 4, 8, C), F32),
            vmem((2, 4, 32, C), BF16),
            pltpu.SemaphoreType.DMA((16,)),
            pltpu.SemaphoreType.DMA((12,)),
            pltpu.SemaphoreType.DMA((12,)),
        ],
        compiler_params=pltpu.CompilerParams(collective_id=0, has_side_effects=True),
        name="atom_layers",
    )(*args)


def solution(mesh):
    in_specs = (P("sample", "atom", None), P("atom", None), P(None, "atom"), P("atom")) + (P(),) * 11
    return jax.shard_map(
        local, mesh=mesh, in_specs=in_specs, out_specs=P("sample", "atom", None), check_vma=False
    )
```

time: 160 us -> 40.2 us (0.25)
  the two profiles are of different devices: /device:TPU:30 before, /device:TPU:6 now
where the time goes in v1:
time: 40.2 us; the launch traced here: 40 us
  Pallas kernels  36.4 us (91%)
  local copies, waits for them, and re-layouts  3.68 us (9%)
    pallas_call x1, Pallas kernels, local(): pl.pallas_call(kernel, out_shape=jax.ShapeDtypeStruct((S, A, C), BF16), i...  36.4 us
    unnamed x5, local copies, waits for them, and re-layouts  3.68 us

profile of v1, /device:TPU:6, one launch (start us, length us, event | category | flops | bytes accessed | tf_op | source)
XLA Modules:
  0.0 40.0 jit_solution(11505808972387215418)
XLA Ops:
  0.0 0.0 copy-start
  0.0 1.4 %copy.16.wpi_h = f32[16,5]{1,0:T(8,128)} copy(f32[16,5]{0,1:T(8,128)} %param.19) | data formatting | bytes 640 | tf_op args[4]
  1.4 0.0 copy-done
  1.4 0.7 %copy.17.wcp_h = bf16[2,128,16]{2,1,0:T(8,128)(2,1)} copy(bf16[2,128,16]{1,2,0:T(8,128)(2,1)S(1)} %copy-done) | data formatting | bytes 16384 | tf_op args[6]
  2.1 36.4 %atom_layers.1 = bf16[2,256,128]{2,1,0:T(8,128)(2,1)} custom-call(bf16[2,256,128]{2,1,0:T(8,128)(2,1)} %act_h.1, bf16[256,128]{1,0:T(8,128)(2,1)} %cond_h.1, f32[3,256]{1,0:T(4,128)} %pos_h.1, s32[1,256]{1,0:T(1,128)} %bitcast.1, f32[16,5]{1,0:T(8,128)} %copy.16.wpi_h, f32[16,9]{1,0:T(8,128)} %wrel_h.1, bf16[2,128,16]{2,1,0:T(8,128)(2,1)} %copy.17.wcp_h, ...), custom_call_target="tpu_custom_call" | custom-call | tf_op jit(solution)/shard_map/atom_layers/pallas_call | solution.py:367
  38.5 1.6 %copy.19 = bf16[2,256,128]{2,1,0:T(8,128)(2,1)} copy(bf16[2,256,128]{2,1,0:T(8,128)(2,1)} %atom_layers.1) | data formatting | bytes 262144
Async XLA Ops:
  0.0 1.4 %copy-start = (bf16[2,128,16]{1,2,0:T(8,128)(2,1)S(1)}, bf16[2,128,16]{1,2,0:T(8,128)(2,1)}, u32[]{:S(2)}) copy-start(bf16[2,128,16]{1,2,0:T(8,128)(2,1)} %param.21) | copy-start | bytes 24580
